TPU v7x, 256 devices: a whole 4x4x8 slice. The times are simulated.
256 devices in a mesh: section: 2 (over core), seq: 16 (over x, y), tensor: 8 (over z).
Axes of the slice: x: 4, y: 4, z: 8, core: 2. Of those that a mesh axis runs over, the one named last changes fastest.
Arguments:
- x_in: bfloat16 [2, 32768, 2048], P(None, 'seq', 'tensor'), may hold values from -6 to 6
- norm_gain: float32 [2, 2048], P('section', 'tensor'), may hold values from 0.5 to 1.5
- right_blocks: bfloat16 [2, 128, 256, 256], P('section', 'seq'), may hold values from -0.375 to 0.375
- left_blocks: bfloat16 [2, 256, 128, 128], P('section', 'seq'), may hold values from -0.5 to 0.5
- gate_first: bfloat16 [2, 32, 64, 64], P('section'), may hold values from -0.75 to 0.75
- gate_second: bfloat16 [2, 64, 32, 32], P('section'), may hold values from -1 to 1
- out_first: bfloat16 [2, 32, 64, 64], P('section'), may hold values from -0.75 to 0.75
- out_second: bfloat16 [2, 64, 32, 32], P('section'), may hold values from -1 to 1
- head: bfloat16 [2, 2048, 32768], P('section', None, ('seq', 'tensor')), may hold values from -0.375 to 0.375
- targets: int32 [2, 256], replicated, may hold values from 0 to 32767
Outputs:
- block_out: bfloat16 [2, 2, 32768, 2048], P('section', None, 'seq', 'tensor')
- aux_losses: float32 [2, 2, 256], P('section')
All inputs are finite; a program needn't handle non-finite values.
Results may differ from a plain program's by a relative error of at most 0.011.
Values may be sent and summed in bfloat16 or wider, within the bound.
No kernel may reach another device: no remote copies, remote signals or barrier semaphores. Data moves between devices by JAX's collectives and lax.ppermute only.
A program may use at most 128 MiB of HBM per device.

v0:
```python
import jax
import jax.numpy as jnp
from jax import lax
from jax.sharding import PartitionSpec as P

C1 = 32
C2 = 64
D = 2048
STRIDE = 128
epsilon = 1e-05


def from_behind(block, axis, distance):
    devices = range(lax.axis_size(axis))
    route = [(i - distance, i) for i in devices if i - distance in devices]
    return lax.ppermute(block, axis, route)


def first_map(factor_local):
    c_one, c_two, _ = factor_local.shape
    identity = jnp.eye(c_one, dtype=factor_local.dtype)
    dense_map = identity[None, :, :, None] * jnp.transpose(factor_local, (1, 0, 2))[:, :, None, :]
    return dense_map.reshape(c_two * c_one, c_one * c_two)


def second_map(factor_local, groups, c_one):
    k_dev = factor_local.shape[0]
    split_view = factor_local.reshape(k_dev, groups, c_one, groups, c_one)
    split_view = jnp.transpose(split_view, (1, 2, 0, 3, 4))
    identity = jnp.eye(k_dev, dtype=factor_local.dtype)
    dense_map = split_view[:, :, :, :, None, :] * identity[None, None, :, None, :, None]
    return dense_map.reshape(groups * c_one * k_dev, groups * k_dev * c_one)


def restore_rows(returned, groups, c_one, k_dev, token_count):
    ordered = returned.reshape(groups, c_one, k_dev, token_count)
    return jnp.transpose(ordered, (3, 1, 0, 2)).reshape(token_count, c_one * groups * k_dev)


def gate_channels(normed, one_map, two_map, groups, c_one, k_dev):
    token_count = normed.shape[0]
    first_mix = jnp.einsum("oc,tc->ot", one_map, normed, preferred_element_type=jnp.float32).astype(
        jnp.bfloat16
    )
    first_mix = first_mix.reshape(groups, k_dev * c_one, token_count)
    incoming = lax.all_to_all(first_mix, "tensor", split_axis=0, concat_axis=0, tiled=True)
    count_here = incoming.shape[2]
    flat_in = incoming.reshape(groups * k_dev * c_one, count_here)
    second_mix = jnp.dot(two_map, flat_in, preferred_element_type=jnp.float32).astype(jnp.bfloat16)
    returned = lax.all_to_all(
        second_mix.reshape(groups, c_one * k_dev, count_here),
        "tensor",
        split_axis=0,
        concat_axis=0,
        tiled=True,
    )
    return restore_rows(returned, groups, c_one, k_dev, token_count)


def out_channels(values, one_map, two_map, groups, c_one, k_dev):
    token_count = values.shape[0]
    first_mix = jnp.einsum("oc,tc->ot", one_map, values, preferred_element_type=jnp.float32).astype(
        jnp.bfloat16
    )
    first_mix = first_mix.reshape(groups, k_dev * c_one, token_count)
    incoming = lax.all_to_all(first_mix, "tensor", split_axis=0, concat_axis=0, tiled=True)
    count_here = incoming.shape[2]
    flat_in = incoming.reshape(groups * k_dev * c_one, count_here)
    second_mix = jnp.dot(two_map, flat_in, preferred_element_type=jnp.float32).astype(jnp.bfloat16)
    returned = lax.all_to_all(
        second_mix.reshape(groups, c_one * k_dev, count_here),
        "tensor",
        split_axis=0,
        concat_axis=0,
        tiled=True,
    )
    return restore_rows(returned, groups, c_one, k_dev, token_count)


def sequence_mix(normed, right_local, left_local, row_count, col_count):
    chan_count = normed.shape[1]
    seq_view = normed.reshape(row_count, col_count, chan_count)
    row_mix = jnp.einsum(
        "pjq,pqc->pjc", right_local, seq_view, preferred_element_type=jnp.float32
    ).astype(jnp.bfloat16)
    col_mix = jnp.einsum(
        "jip,pjc->ijc",
        left_local,
        lax.all_to_all(row_mix, "seq", split_axis=1, concat_axis=0, tiled=True),
        preferred_element_type=jnp.float32,
    ).astype(jnp.bfloat16)
    returned = lax.all_to_all(col_mix, "seq", split_axis=0, concat_axis=1, tiled=True)
    return returned.reshape(row_count * col_count, chan_count)


def body(
    x_in,
    norm_gain,
    right_blocks,
    left_blocks,
    gate_first,
    gate_second,
    out_first,
    out_second,
    head,
    targets,
):
    section_index = lax.axis_index("section")
    tensor_count = lax.axis_size("tensor")
    tensor_index = lax.axis_index("tensor")
    micro_count = x_in.shape[0]
    tok_dev = x_in.shape[1]
    chan_dev = x_in.shape[2]
    row_count = right_blocks.shape[1]
    col_count = right_blocks.shape[2]
    c_one = C1 // tensor_count
    k_dev = C2 // tensor_count
    norm_scale = norm_gain[0]
    right_local = right_blocks[0]
    left_local = left_blocks[0]
    gate_first_all = gate_first[0]
    gate_second_all = gate_second[0]
    out_first_all = out_first[0]
    out_second_all = out_second[0]
    gate_one = first_map(lax.dynamic_slice_in_dim(gate_first_all, tensor_index * c_one, c_one, 0))
    gate_two = second_map(
        lax.dynamic_slice_in_dim(gate_second_all, tensor_index * k_dev, k_dev, 0),
        tensor_count,
        c_one,
    )
    out_one = first_map(lax.dynamic_slice_in_dim(out_first_all, tensor_index * c_one, c_one, 0))
    out_two = second_map(
        lax.dynamic_slice_in_dim(out_second_all, tensor_index * k_dev, k_dev, 0),
        tensor_count,
        c_one,
    )
    head_local = head[0]
    vocab_dev = head_local.shape[1]
    vocab_offset = lax.axis_index(("seq", "tensor")) * vocab_dev
    handed = jnp.zeros((tok_dev, chan_dev), jnp.bfloat16)
    first_outputs, second_outputs, first_losses, second_losses = ([], [], [], [])
    for step_index in range(micro_count + 1):
        feed_rows = x_in[min(step_index, micro_count - 1)]
        x_val = jnp.where(section_index == 0, feed_rows, handed)
        labels = jnp.where(
            section_index == 0,
            targets[min(step_index, micro_count - 1)],
            targets[max(step_index - 1, 0)],
        )
        x_float = x_val.astype(jnp.float32)
        square_part = jnp.sum(x_float * x_float, axis=1)
        square_total = lax.psum(square_part, "tensor")
        row_scale = lax.rsqrt(square_total / D + epsilon)
        normed = (x_float * row_scale[:, None] * norm_scale[None, :]).astype(jnp.bfloat16)
        seq_out = sequence_mix(normed, right_local, left_local, row_count, col_count)
        gate_pre = gate_channels(normed, gate_one, gate_two, tensor_count, c_one, k_dev)
        gated_mix = (
            seq_out.astype(jnp.float32) * jax.nn.sigmoid(gate_pre.astype(jnp.float32))
        ).astype(jnp.bfloat16)
        out_pre = out_channels(gated_mix, out_one, out_two, tensor_count, c_one, k_dev)
        result = (x_float + out_pre.astype(jnp.float32)).astype(jnp.bfloat16)
        scored = result.reshape(row_count, col_count, chan_dev)[:, ::STRIDE, :].reshape(
            -1, chan_dev
        )
        wide_rows = lax.all_gather(scored, "tensor", axis=1, tiled=True)
        logits = jnp.dot(
            lax.all_gather(wide_rows, "seq", axis=0, tiled=True),
            head_local,
            preferred_element_type=jnp.float32,
        )
        exp_sums = jnp.sum(jnp.exp(logits), axis=1)
        vocab_ids = jnp.arange(vocab_dev, dtype=jnp.int32)[None, :] + vocab_offset
        is_target = vocab_ids == labels[:, None]
        target_part = jnp.sum(jnp.where(is_target, logits, 0.0), axis=1)
        exp_total, target_logit = lax.psum((exp_sums, target_part), ("seq", "tensor"))
        result, aux_loss = (result, jnp.log(exp_total) - target_logit)
        if step_index < micro_count:
            first_outputs.append(result)
            first_losses.append(aux_loss)
            handed = from_behind(result, "section", 1)
        if step_index > 0:
            second_outputs.append(result)
            second_losses.append(aux_loss)
    block_out = jnp.where(section_index == 0, jnp.stack(first_outputs), jnp.stack(second_outputs))[
        None
    ]
    aux_losses = jnp.where(section_index == 0, jnp.stack(first_losses), jnp.stack(second_losses))[
        None
    ]
    return (block_out, aux_losses)


def solution(mesh):
    in_specs = (
        P(None, "seq", "tensor"),
        P("section", "tensor"),
        P("section", "seq", None, None),
        P("section", "seq", None, None),
        P("section", None, None, None),
        P("section", None, None, None),
        P("section", None, None, None),
        P("section", None, None, None),
        P("section", None, ("seq", "tensor")),
        P(),
    )
    out_specs = (P("section", None, "seq", "tensor"), P("section", None, None))
    return jax.shard_map(body, mesh=mesh, in_specs=in_specs, out_specs=out_specs, check_vma=False)
```

profile of v0, /device:TPU:0, one launch (start us, length us, event | category | flops | bytes accessed | tf_op | source)
XLA Modules:
  0.0 1093.3 jit_solution(17827740526057056564)
XLA Ops:
  13.2 18.5 %psum.63 = f32[2048]{0:T(1024)S(1)} all-reduce(f32[2048]{0:T(1024)S(1)} %fusion.18), channel_id=1, replica_groups=mesh['section'=2,'seq'=16,'tensor'=8] {'tensor'}, use_global_device_ids=true, to_apply=%region_1.2 | all-reduce | flops 2048 | bytes 16384 | tf_op jit(solution)/shard_map/psum | solution.py:152
  43.1 19.9 %all-to-all-done.2 = bf16[8,32,2048]{2,1,0:T(8,128)(2,1)} async-done(((bf16[8,32,2048]{2,1,0:T(8,128)(2,1)}), bf16[8,32,2048]{2,1,0:T(8,128)(2,1)}, u32[]{:S(2)}, u32[]{:S(2)}) %all-to-all-start.2) | async-done | bytes 1048608 | tf_op jit(solution)/shard_map/all_to_all | solution.py:46
  63.0 7.1 all-to-all-start
  93.4 17.9 %all-to-all-done.3 = bf16[8,32,2048]{2,1,0:T(8,128)(2,1)S(1)} async-done(((bf16[8,32,2048]{2,1,0:T(8,128)(2,1)}), bf16[8,32,2048]{2,1,0:T(8,128)(2,1)S(1)}, u32[]{:S(2)}, u32[]{:S(2)}) %all-to-all-start.3) | async-done | bytes 1048608 | tf_op jit(solution)/shard_map/all_to_all | solution.py:50
  117.2 9.1 reshape.474
  126.3 11.8 %copy.100 = f32[8,16,16,256]{3,2,0,1:T(8,128)S(1)} copy(f32[8,16,16,256]{2,1,0,3:T(8,128)} %reshape.474) | data formatting | bytes 4194304 | tf_op jit(solution)/shard_map/div | solution.py:158
  148.3 22.9 %all-to-all-done.4 = bf16[8,32,2048]{2,1,0:T(8,128)(2,1)} async-done(((bf16[8,32,2048]{2,1,0:T(8,128)(2,1)}), bf16[8,32,2048]{2,1,0:T(8,128)(2,1)}, u32[]{:S(2)}, u32[]{:S(2)}) %all-to-all-start.4) | async-done | bytes 1048608 | tf_op jit(solution)/shard_map/all_to_all | solution.py:66
  172.9 28.1 %all_to_all.141 = bf16[8,32,2048]{2,1,0:T(8,128)(2,1)S(1)} all-to-all(bf16[8,32,2048]{2,1,0:T(8,128)(2,1)S(1)} %bitcast.255), channel_id=1, replica_groups=mesh['section'=2,'seq'=16,'tensor'=8] {'tensor'}, dimensions={0} | all-to-all | bytes 2097152 | tf_op jit(solution)/shard_map/all_to_all | solution.py:70
  211.0 14.9 %psum.64 = f32[2048]{0:T(1024)S(1)} all-reduce(f32[2048]{0:T(1024)S(1)} %get-tuple-element.22), channel_id=1, replica_groups=mesh['section'=2,'seq'=16,'tensor'=8] {'tensor'}, use_global_device_ids=true, to_apply=%region_3.4 | all-reduce | flops 2048 | bytes 16384 | tf_op jit(solution)/shard_map/psum | solution.py:152
  239.5 20.1 %all-to-all-done.8 = bf16[8,32,2048]{2,1,0:T(8,128)(2,1)} async-done(((bf16[8,32,2048]{2,1,0:T(8,128)(2,1)}), bf16[8,32,2048]{2,1,0:T(8,128)(2,1)}, u32[]{:S(2)}, u32[]{:S(2)}) %all-to-all-start.8) | async-done | bytes 1048608 | tf_op jit(solution)/shard_map/all_to_all | solution.py:46
  259.6 7.0 all-to-all-start.6
  269.3 11.2 %all-to-all-done.6 = bf16[8,256,256]{2,0,1:T(8,128)(2,1)} async-done(((bf16[8,256,256]{2,0,1:T(8,128)(2,1)}), bf16[8,256,256]{2,0,1:T(8,128)(2,1)}, u32[]{:S(2)}, u32[]{:S(2)}) %all-to-all-start.6) | async-done | bytes 1048608 | tf_op jit(solution)/shard_map/all_to_all | solution.py:89
  290.5 17.9 %all-to-all-done.9 = bf16[8,32,2048]{2,1,0:T(8,128)(2,1)} async-done(((bf16[8,32,2048]{2,1,0:T(8,128)(2,1)}), bf16[8,32,2048]{2,1,0:T(8,128)(2,1)}, u32[]{:S(2)}, u32[]{:S(2)}) %all-to-all-start.9) | async-done | bytes 1048608 | tf_op jit(solution)/shard_map/all_to_all | solution.py:50
  316.3 10.4 reshape.479
  326.8 12.9 %copy.112 = f32[8,16,16,256]{3,2,0,1:T(8,128)} copy(f32[8,16,16,256]{2,1,0,3:T(8,128)} %reshape.479) | data formatting | bytes 4194304 | tf_op jit(solution)/shard_map/div | solution.py:158
  342.4 28.1 %all_to_all.142 = bf16[8,32,2048]{2,1,0:T(8,128)(2,1)S(1)} all-to-all(bf16[8,32,2048]{2,1,0:T(8,128)(2,1)S(1)} %bitcast.258), channel_id=1, replica_groups=mesh['section'=2,'seq'=16,'tensor'=8] {'tensor'}, dimensions={0} | all-to-all | bytes 2097152 | tf_op jit(solution)/shard_map/all_to_all | solution.py:66
  371.0 27.4 %all_to_all.143 = bf16[8,32,2048]{2,1,0:T(8,128)(2,1)S(1)} all-to-all(bf16[8,32,2048]{2,1,0:T(8,128)(2,1)S(1)} %bitcast.260), channel_id=1, replica_groups=mesh['section'=2,'seq'=16,'tensor'=8] {'tensor'}, dimensions={0} | all-to-all | bytes 2097152 | tf_op jit(solution)/shard_map/all_to_all | solution.py:70
  405.1 15.0 %psum.65 = f32[2048]{0:T(1024)S(1)} all-reduce(f32[2048]{0:T(1024)S(1)} %get-tuple-element.20), channel_id=1, replica_groups=mesh['section'=2,'seq'=16,'tensor'=8] {'tensor'}, use_global_device_ids=true, to_apply=%region_5.6 | all-reduce | flops 2048 | bytes 16384 | tf_op jit(solution)/shard_map/psum | solution.py:152
  433.7 20.5 %all-to-all-done.14 = bf16[8,32,2048]{2,1,0:T(8,128)(2,1)} async-done(((bf16[8,32,2048]{2,1,0:T(8,128)(2,1)}), bf16[8,32,2048]{2,1,0:T(8,128)(2,1)}, u32[]{:S(2)}, u32[]{:S(2)}) %all-to-all-start.14) | async-done | bytes 1048608 | tf_op jit(solution)/shard_map/all_to_all | solution.py:46
  454.1 6.9 all-to-all-start.12
  463.7 11.3 %all-to-all-done.12 = bf16[8,256,256]{2,0,1:T(8,128)(2,1)} async-done(((bf16[8,256,256]{2,0,1:T(8,128)(2,1)}), bf16[8,256,256]{2,0,1:T(8,128)(2,1)}, u32[]{:S(2)}, u32[]{:S(2)}) %all-to-all-start.12) | async-done | bytes 1048608 | tf_op jit(solution)/shard_map/all_to_all | solution.py:89
  484.9 18.1 %all-to-all-done.15 = bf16[8,32,2048]{2,1,0:T(8,128)(2,1)} async-done(((bf16[8,32,2048]{2,1,0:T(8,128)(2,1)}), bf16[8,32,2048]{2,1,0:T(8,128)(2,1)}, u32[]{:S(2)}, u32[]{:S(2)}) %all-to-all-start.15) | async-done | bytes 1048608 | tf_op jit(solution)/shard_map/all_to_all | solution.py:50
  511.0 10.4 reshape.483
  521.4 12.9 %copy.122 = f32[8,16,16,256]{3,2,0,1:T(8,128)} copy(f32[8,16,16,256]{2,1,0,3:T(8,128)} %reshape.483) | data formatting | bytes 4194304 | tf_op jit(solution)/shard_map/div | solution.py:158
  545.2 6.3 slice.28
  553.0 32.3 %all_gather.18 = bf16[16,2048]{1,0:T(8,128)(2,1)} all-gather(bf16[16,256]{1,0:T(8,128)(2,1)S(1)} %reshape.465), channel_id=1, replica_groups=mesh['section'=2,'seq'=16,'tensor'=8] {'tensor'}, dimensions={1}, use_global_device_ids=true | all-gather | bytes 73728 | tf_op jit(solution)/shard_map/all_gather | solution.py:165
  587.9 5.8 all-to-all-start.17
  597.3 35.3 %all_gather.20 = bf16[16,2048]{1,0:T(8,128)(2,1)} all-gather(bf16[16,256]{1,0:T(8,128)(2,1)S(1)} %reshape.467), channel_id=1, replica_groups=mesh['section'=2,'seq'=16,'tensor'=8] {'tensor'}, dimensions={1}, use_global_device_ids=true | all-gather | bytes 73728 | tf_op jit(solution)/shard_map/all_gather | solution.py:165
  640.3 26.5 %all_gather.22 = bf16[16,2048]{1,0:T(8,128)(2,1)} all-gather(bf16[16,256]{1,0:T(8,128)(2,1)S(1)} %reshape.469), channel_id=1, replica_groups=mesh['section'=2,'seq'=16,'tensor'=8] {'tensor'}, dimensions={1}, use_global_device_ids=true | all-gather | bytes 73728 | tf_op jit(solution)/shard_map/all_gather | solution.py:165
  671.7 11.2 %all-gather.6.cloned.1.call-done = bf16[256,2048]{1,0:T(8,128)(2,1)} async-done(((bf16[16,2048]{1,0:T(8,128)(2,1)}), bf16[256,2048]{1,0:T(8,128)(2,1)}) %all-gather.6.cloned.1.call-update) | async-done | bytes 1048592 | tf_op jit(solution)/shard_map/all_gather | solution.py:167
  691.5 40.9 %all-gather.8.cloned.1.call-done = bf16[256,2048]{1,0:T(8,128)(2,1)} async-done(((bf16[16,2048]{1,0:T(8,128)(2,1)}), bf16[256,2048]{1,0:T(8,128)(2,1)}) %all-gather.8.cloned.1.call-update) | async-done | bytes 1048592 | tf_op jit(solution)/shard_map/all_gather | solution.py:167
  734.2 351.8 %all-reduce = (f32[256]{0:T(256)S(1)}, f32[256]{0:T(256)S(1)}, f32[256]{0:T(256)S(1)}, f32[256]{0:T(256)S(1)}, f32[256]{0:T(256)S(1)}, /*index=5*/f32[256]{0:T(256)S(1)}) all-reduce(f32[256]{0:T(256)S(1)} %get-tuple-element.30, f32[256]{0:T(256)S(1)} %get-tuple-element.31, ...), channel_id=1, replica_groups=mesh['section'=2,'seq'=16,'tensor'=8] {'seq','tensor'}, use_global_device_ids=true, to_apply=%region_13.14 | all-reduce | flops 1536 | bytes 12288 | tf_op jit(solution)/shard_map/psum | solution.py:175
  (184 shorter events, 188.5 us)
Async XLA Ops:
  7.2 31.8 %copy-start = (bf16[1,8,256,256]{3,2,1,0:T(8,128)(2,1)S(1)}, bf16[1,8,256,256]{3,2,1,0:T(8,128)(2,1)}, u32[]{:S(2)}) copy-start(bf16[1,8,256,256]{3,2,1,0:T(8,128)(2,1)} %param.12) | copy-start | bytes 3145732
  9.5 22.2 %copy-start.19 = (bf16[256,256]{1,0:T(8,128)(2,1)}, bf16[256,256]{1,0:T(8,128)(2,1)S(1)}, u32[]{:S(2)}) copy-start(bf16[256,256]{1,0:T(8,128)(2,1)S(1)} %mul.236) | copy-start | bytes 393220
  12.3 19.5 %copy-start.26 = (f32[1,256]{1,0:T(1,128)S(1)}, f32[1,256]{1,0:T(1,128)}, u32[]{:S(2)}) copy-start(f32[1,256]{1,0:T(1,128)} %param.11) | copy-start | bytes 3076
  12.9 24.6 %copy-start.1 = (bf16[1,2048,256]{1,2,0:T(8,128)(2,1)}, bf16[1,2048,256]{1,2,0:T(8,128)(2,1)S(1)}, u32[]{:S(2)}) copy-start(bf16[1,2048,256]{1,2,0:T(8,128)(2,1)S(1)} %copy.135) | copy-start | bytes 3145732
  33.3 29.7 %all-to-all-start.2 = ((bf16[8,32,2048]{2,1,0:T(8,128)(2,1)}), bf16[8,32,2048]{2,1,0:T(8,128)(2,1)}, u32[]{:S(2)}, u32[]{:S(2)}) async-start(bf16[8,32,2048]{2,1,0:T(8,128)(2,1)} %bitcast.21), calls=%async_computation.2 | async-start | bytes 2097152 | tf_op jit(solution)/shard_map/all_to_all | solution.py:46
  40.4 29.7 %copy-start.24 = (bf16[1,64,32,32]{1,3,2,0:T(8,128)(2,1)S(1)}, bf16[1,64,32,32]{1,3,2,0:T(8,128)(2,1)}, u32[]{:S(2)}) copy-start(bf16[1,64,32,32]{1,3,2,0:T(8,128)(2,1)} %param.15) | copy-start | bytes 393220
  43.1 27.0 %copy-start.25 = (bf16[1,64,32,32]{1,3,2,0:T(8,128)(2,1)S(1)}, bf16[1,64,32,32]{1,3,2,0:T(8,128)(2,1)}, u32[]{:S(2)}) copy-start(bf16[1,64,32,32]{1,3,2,0:T(8,128)(2,1)} %param.17) | copy-start | bytes 393220
  63.0 21.0 %all-to-all-start = ((bf16[8,256,256]{2,0,1:T(8,128)(2,1)}), bf16[8,256,256]{2,0,1:T(8,128)(2,1)}, u32[]{:S(2)}, u32[]{:S(2)}) async-start(bf16[8,256,256]{2,0,1:T(8,128)(2,1)} %copy.92), calls=%async_computation | async-start | bytes 2097152 | tf_op jit(solution)/shard_map/all_to_all | solution.py:89
  84.0 27.3 %all-to-all-start.3 = ((bf16[8,32,2048]{2,1,0:T(8,128)(2,1)}), bf16[8,32,2048]{2,1,0:T(8,128)(2,1)S(1)}, u32[]{:S(2)}, u32[]{:S(2)}) async-start(bf16[8,32,2048]{2,1,0:T(8,128)(2,1)} %bitcast.247), calls=%async_computation.3 | async-start | bytes 2097152 | tf_op jit(solution)/shard_map/all_to_all | solution.py:50
  90.7 25.6 %copy-start.22 = (bf16[64,4,4,64]{3,2,1,0:T(4,128)(2,1)S(1)}, bf16[64,4,4,64]{3,2,1,0:T(4,128)(2,1)}, u32[]{:S(2)}) copy-start(bf16[64,4,4,64]{3,2,1,0:T(4,128)(2,1)} %get-tuple-element.35) | copy-start | bytes 393220
  111.3 26.8 %all-to-all-start.1 = ((bf16[128,16,256]{2,1,0:T(8,128)(2,1)}), bf16[128,16,256]{2,1,0:T(8,128)(2,1)}, u32[]{:S(2)}, u32[]{:S(2)}) async-start(bf16[128,16,256]{2,1,0:T(8,128)(2,1)} %copy.96), calls=%async_computation.1 | async-start | bytes 2097152 | tf_op jit(solution)/shard_map/all_to_all | solution.py:92
  141.2 30.0 %all-to-all-start.4 = ((bf16[8,32,2048]{2,1,0:T(8,128)(2,1)}), bf16[8,32,2048]{2,1,0:T(8,128)(2,1)}, u32[]{:S(2)}, u32[]{:S(2)}) async-start(bf16[8,32,2048]{2,1,0:T(8,128)(2,1)} %bitcast.250), calls=%async_computation.4 | async-start | bytes 2097152 | tf_op jit(solution)/shard_map/all_to_all | solution.py:66
  203.7 4.6 collective-permute-start
  229.9 29.7 %all-to-all-start.8 = ((bf16[8,32,2048]{2,1,0:T(8,128)(2,1)}), bf16[8,32,2048]{2,1,0:T(8,128)(2,1)}, u32[]{:S(2)}, u32[]{:S(2)}) async-start(bf16[8,32,2048]{2,1,0:T(8,128)(2,1)} %bitcast.251), calls=%async_computation.8 | async-start | bytes 2097152 | tf_op jit(solution)/shard_map/all_to_all | solution.py:46
  259.6 20.8 %all-to-all-start.6 = ((bf16[8,256,256]{2,0,1:T(8,128)(2,1)}), bf16[8,256,256]{2,0,1:T(8,128)(2,1)}, u32[]{:S(2)}, u32[]{:S(2)}) async-start(bf16[8,256,256]{2,0,1:T(8,128)(2,1)} %copy.106), calls=%async_computation.6 | async-start | bytes 2097152 | tf_op jit(solution)/shard_map/all_to_all | solution.py:89
  280.5 27.9 %all-to-all-start.9 = ((bf16[8,32,2048]{2,1,0:T(8,128)(2,1)}), bf16[8,32,2048]{2,1,0:T(8,128)(2,1)}, u32[]{:S(2)}, u32[]{:S(2)}) async-start(bf16[8,32,2048]{2,1,0:T(8,128)(2,1)} %bitcast.248), calls=%async_computation.9 | async-start | bytes 2097152 | tf_op jit(solution)/shard_map/all_to_all | solution.py:50
  308.4 31.3 %all-to-all-start.7 = ((bf16[128,16,256]{2,1,0:T(8,128)(2,1)}), bf16[128,16,256]{2,1,0:T(8,128)(2,1)}, u32[]{:S(2)}, u32[]{:S(2)}) async-start(bf16[128,16,256]{2,1,0:T(8,128)(2,1)} %copy.110), calls=%async_computation.7 | async-start | bytes 2097152 | tf_op jit(solution)/shard_map/all_to_all | solution.py:92
  400.1 3.6 collective-permute-start.1
  424.1 30.1 %all-to-all-start.14 = ((bf16[8,32,2048]{2,1,0:T(8,128)(2,1)}), bf16[8,32,2048]{2,1,0:T(8,128)(2,1)}, u32[]{:S(2)}, u32[]{:S(2)}) async-start(bf16[8,32,2048]{2,1,0:T(8,128)(2,1)} %bitcast.249), calls=%async_computation.14 | async-start | bytes 2097152 | tf_op jit(solution)/shard_map/all_to_all | solution.py:46
  454.1 20.8 %all-to-all-start.12 = ((bf16[8,256,256]{2,0,1:T(8,128)(2,1)}), bf16[8,256,256]{2,0,1:T(8,128)(2,1)}, u32[]{:S(2)}, u32[]{:S(2)}) async-start(bf16[8,256,256]{2,0,1:T(8,128)(2,1)} %copy.116), calls=%async_computation.12 | async-start | bytes 2097152 | tf_op jit(solution)/shard_map/all_to_all | solution.py:89
  474.9 28.1 %all-to-all-start.15 = ((bf16[8,32,2048]{2,1,0:T(8,128)(2,1)}), bf16[8,32,2048]{2,1,0:T(8,128)(2,1)}, u32[]{:S(2)}, u32[]{:S(2)}) async-start(bf16[8,32,2048]{2,1,0:T(8,128)(2,1)} %bitcast.246), calls=%async_computation.15 | async-start | bytes 2097152 | tf_op jit(solution)/shard_map/all_to_all | solution.py:50
  503.0 31.3 %all-to-all-start.13 = ((bf16[128,16,256]{2,1,0:T(8,128)(2,1)}), bf16[128,16,256]{2,1,0:T(8,128)(2,1)}, u32[]{:S(2)}, u32[]{:S(2)}) async-start(bf16[128,16,256]{2,1,0:T(8,128)(2,1)} %copy.120), calls=%async_computation.13 | async-start | bytes 2097152 | tf_op jit(solution)/shard_map/all_to_all | solution.py:92
  538.1 47.2 %all-to-all-start.16 = ((bf16[8,32,2048]{2,1,0:T(8,128)(2,1)}), bf16[8,32,2048]{2,1,0:T(8,128)(2,1)}, u32[]{:S(2)}, u32[]{:S(2)}) async-start(bf16[8,32,2048]{2,1,0:T(8,128)(2,1)} %bitcast.244), calls=%async_computation.16 | async-start | bytes 2097152 | tf_op jit(solution)/shard_map/all_to_all | solution.py:66
  542.3 127.1 %all-gather.4.cloned.1.call-start = ((), (), s32[]{:S(2)}) async-start(), calls=%async_computation.18 | async-start | bytes 1114112 | tf_op jit(solution)/shard_map/all_gather | solution.py:167
  587.9 44.8 %all-to-all-start.17 = ((bf16[8,32,2048]{2,1,0:T(8,128)(2,1)}), bf16[8,32,2048]{2,1,0:T(8,128)(2,1)}, u32[]{:S(2)}, u32[]{:S(2)}) async-start(bf16[8,32,2048]{2,1,0:T(8,128)(2,1)} %bitcast.245), calls=%async_computation.17 | async-start | bytes 2097152 | tf_op jit(solution)/shard_map/all_to_all | solution.py:70
  593.7 89.2 %all-gather.6.cloned.1.call-start = ((), (), s32[]{:S(2)}) async-start(), calls=%async_computation.19 | async-start | bytes 1114112 | tf_op jit(solution)/shard_map/all_gather | solution.py:167
  632.7 99.7 %all-gather.8.cloned.1.call-start = ((), (), s32[]{:S(2)}) async-start(), calls=%async_computation.20 | async-start | bytes 1114112 | tf_op jit(solution)/shard_map/all_gather | solution.py:167
  636.7 30.1 %copy-start.27 = (s32[2,256]{1,0:T(2,128)S(1)}, s32[2,256]{1,0:T(2,128)}, u32[]{:S(2)}) copy-start(s32[2,256]{1,0:T(2,128)} %param.19) | copy-start | bytes 6148
  669.4 16.4 %copy-start.11 = (bf16[2048,256]{0,1:T(8,128)(2,1)S(1)}, bf16[2048,256]{0,1:T(8,128)(2,1)}, u32[]{:S(2)}) copy-start(bf16[2048,256]{0,1:T(8,128)(2,1)} %copy-done.10) | copy-start | bytes 3145732
  669.4 16.4 %copy-start.12 = (bf16[2048,256]{0,1:T(8,128)(2,1)S(1)}, bf16[2048,256]{0,1:T(8,128)(2,1)}, u32[]{:S(2)}) copy-start(bf16[2048,256]{0,1:T(8,128)(2,1)} %fusion.7) | copy-start | bytes 3145732
  687.4 44.9 %copy-start.17 = (bf16[1,2048,256]{2,1,0:T(8,128)(2,1)S(1)}, bf16[1,2048,256]{2,1,0:T(8,128)(2,1)}, u32[]{:S(2)}) copy-start(bf16[1,2048,256]{2,1,0:T(8,128)(2,1)} %param.18) | copy-start | bytes 3145732
  687.4 44.9 %copy-start.23 = (f32[256,256]{0,1:T(8,128)S(1)}, f32[256,256]{0,1:T(8,128)}, u32[]{:S(2)}) copy-start(f32[256,256]{0,1:T(8,128)} %fusion.34) | copy-start | bytes 786436
  (16 other events, 39.9 us)
Sparse Core Ops, SparseCore 0:
  585.4 47.9 all-gather.3
  635.8 47.0 all-gather.5
  685.3 47.0 all-gather.7
where the time goes:
time: 1100 us; the launch traced here: 1090 us
  blocking collectives  578 us (53%)
  waiting for transfers between devices  219 us (20%)
  local copies, waits for them, and re-layouts  132 us (12%)
  starting transfers between devices  78.2 us (7%)
  matrix products  38.8 us (4%)
  other arithmetic  32.9 us (3%)
  between operations  14.8 us (1%)
    psum x1, blocking collectives, body(): lax.psum((exp_sums, target_part), ('seq', 'tensor'))  352 us
    all_gather x3, blocking collectives, body(): wide_rows = lax.all_gather(scored, 'tensor', axis=1, tiled=True)  94.1 us
    div x9, local copies, waits for them, and re-layouts, body(): jax.nn.sigmoid(gate_pre.astype(jnp.float32))  70.5 us
    all_to_all x3, waiting for transfers between devices, gate_channels(): lax.all_to_all(first_mix, 'tensor', split_axis=0, concat_axis=0, tiled=True)  60.5 us
    all_to_all x2, blocking collectives, out_channels(): lax.all_to_all(second_mix.reshape(groups, c_one * k_dev, count_here), 'te...  55.5 us
    all_to_all x3, waiting for transfers between devices, gate_channels(): lax.all_to_all(second_mix.reshape(groups, c_one * k_dev, count_here), 'te...  53.8 us
    all_gather x3, waiting for transfers between devices, body(): lax.all_gather(wide_rows, 'seq', axis=0, tiled=True)  52.1 us
    psum x3, blocking collectives, body(): square_total = lax.psum(square_part, 'tensor')  48.4 us
  transfers between devices with their start and end apart: 20, of which 13 were waited for; matrix products, arithmetic and copies ran while one was open for 15% of the time, Pallas kernels for 0%

commit v1 on v0

--- a/solution.py
+++ b/solution.py
@@ -172,7 +172,13 @@
         vocab_ids = jnp.arange(vocab_dev, dtype=jnp.int32)[None, :] + vocab_offset
         is_target = vocab_ids == labels[:, None]
         target_part = jnp.sum(jnp.where(is_target, logits, 0.0), axis=1)
-        exp_total, target_logit = lax.psum((exp_sums, target_part), ("seq", "tensor"))
+
+        def shape_rounds_for(inputs):
+            for k in ("seq", "tensor"):
+                inputs = lax.psum(inputs, axis_name=k)
+            return inputs
+
+        exp_total, target_logit = shape_rounds_for((exp_sums, target_part))
         result, aux_loss = (result, jnp.log(exp_total) - target_logit)
         if step_index < micro_count:
             first_outputs.append(result)

time: 1100 us -> 809 us (0.74)
  blocking collectives: 578 us -> 282 us
    psum x1 -> x2, blocking collectives: 352 us -> 56.4 us  [shape_rounds_for(): inputs = lax.psum(inputs, axis_name=k)]
  transfers between devices with their start and end apart: 20 -> 20, of which waited for: 13 -> 13; matrix products, arithmetic and copies ran while one was open for 15% -> 20% of each run, Pallas kernels for 0% -> 0%
where the time goes in v1:
time: 809 us; the launch traced here: 798 us
  blocking collectives  282 us (35%)
  waiting for transfers between devices  220 us (27%)
  local copies, waits for them, and re-layouts  132 us (16%)
  starting transfers between devices  78.2 us (10%)
  matrix products  38.8 us (5%)
  other arithmetic  32.8 us (4%)
  between operations  14.8 us (2%)
    all_gather x3, blocking collectives, body(): wide_rows = lax.all_gather(scored, 'tensor', axis=1, tiled=True)  93.8 us
    div x9, local copies, waits for them, and re-layouts, body(): jax.nn.sigmoid(gate_pre.astype(jnp.float32))  70.5 us
    all_to_all x3, waiting for transfers between devices, gate_channels(): lax.all_to_all(first_mix, 'tensor', split_axis=0, concat_axis=0, tiled=True)  60.6 us
    psum x2, blocking collectives, shape_rounds_for(): inputs = lax.psum(inputs, axis_name=k)  56.4 us
    all_to_all x2, blocking collectives, out_channels(): lax.all_to_all(second_mix.reshape(groups, c_one * k_dev, count_here), 'te...  55.5 us
    all_to_all x3, waiting for transfers between devices, gate_channels(): lax.all_to_all(second_mix.reshape(groups, c_one * k_dev, count_here), 'te...  53.8 us
    all_gather x3, waiting for transfers between devices, body(): lax.all_gather(wide_rows, 'seq', axis=0, tiled=True)  52.5 us
    psum x3, blocking collectives, body(): square_total = lax.psum(square_part, 'tensor')  48.4 us
  transfers between devices with their start and end apart: 20, of which 13 were waited for; matrix products, arithmetic and copies ran while one was open for 20% of the time, Pallas kernels for 0%

profile of v1, /device:TPU:0, one launch (start us, length us, event | category | flops | bytes accessed | tf_op | source)
XLA Modules:
  0.0 797.9 jit_solution(1166024801991567434)
XLA Ops:
  13.2 18.5 %psum.105 = f32[2048]{0:T(1024)S(1)} all-reduce(f32[2048]{0:T(1024)S(1)} %fusion.18), channel_id=1, replica_groups=mesh['section'=2,'seq'=16,'tensor'=8] {'tensor'}, use_global_device_ids=true, to_apply=%region_1.2 | all-reduce | flops 2048 | bytes 16384 | tf_op jit(solution)/shard_map/psum | solution.py:152
  43.1 19.9 %all-to-all-done.2 = bf16[8,32,2048]{2,1,0:T(8,128)(2,1)} async-done(((bf16[8,32,2048]{2,1,0:T(8,128)(2,1)}), bf16[8,32,2048]{2,1,0:T(8,128)(2,1)}, u32[]{:S(2)}, u32[]{:S(2)}) %all-to-all-start.2) | async-done | bytes 1048608 | tf_op jit(solution)/shard_map/all_to_all | solution.py:46
  63.0 7.1 all-to-all-start
  93.4 17.9 %all-to-all-done.3 = bf16[8,32,2048]{2,1,0:T(8,128)(2,1)S(1)} async-done(((bf16[8,32,2048]{2,1,0:T(8,128)(2,1)}), bf16[8,32,2048]{2,1,0:T(8,128)(2,1)S(1)}, u32[]{:S(2)}, u32[]{:S(2)}) %all-to-all-start.3) | async-done | bytes 1048608 | tf_op jit(solution)/shard_map/all_to_all | solution.py:50
  117.2 9.1 %reshape.474 = f32[8,16,16,256]{2,1,0,3:T(8,128)} reshape(f32[2048,4,8,8]{0,3,2,1:T(8,128)S(1)} %copy.99) | data formatting | bytes 4194304 | tf_op jit(solution)/shard_map/div | solution.py:158
  126.2 11.8 %copy.100 = f32[8,16,16,256]{3,2,0,1:T(8,128)S(1)} copy(f32[8,16,16,256]{2,1,0,3:T(8,128)} %reshape.474) | data formatting | bytes 4194304 | tf_op jit(solution)/shard_map/div | solution.py:158
  148.3 22.9 %all-to-all-done.4 = bf16[8,32,2048]{2,1,0:T(8,128)(2,1)} async-done(((bf16[8,32,2048]{2,1,0:T(8,128)(2,1)}), bf16[8,32,2048]{2,1,0:T(8,128)(2,1)}, u32[]{:S(2)}, u32[]{:S(2)}) %all-to-all-start.4) | async-done | bytes 1048608 | tf_op jit(solution)/shard_map/all_to_all | solution.py:66
  172.8 28.1 %all_to_all.141 = bf16[8,32,2048]{2,1,0:T(8,128)(2,1)S(1)} all-to-all(bf16[8,32,2048]{2,1,0:T(8,128)(2,1)S(1)} %bitcast.255), channel_id=1, replica_groups=mesh['section'=2,'seq'=16,'tensor'=8] {'tensor'}, dimensions={0} | all-to-all | bytes 2097152 | tf_op jit(solution)/shard_map/all_to_all | solution.py:70
  210.9 14.9 %psum.106 = f32[2048]{0:T(1024)S(1)} all-reduce(f32[2048]{0:T(1024)S(1)} %get-tuple-element.28), channel_id=1, replica_groups=mesh['section'=2,'seq'=16,'tensor'=8] {'tensor'}, use_global_device_ids=true, to_apply=%region_3.4 | all-reduce | flops 2048 | bytes 16384 | tf_op jit(solution)/shard_map/psum | solution.py:152
  239.4 20.2 %all-to-all-done.8 = bf16[8,32,2048]{2,1,0:T(8,128)(2,1)} async-done(((bf16[8,32,2048]{2,1,0:T(8,128)(2,1)}), bf16[8,32,2048]{2,1,0:T(8,128)(2,1)}, u32[]{:S(2)}, u32[]{:S(2)}) %all-to-all-start.8) | async-done | bytes 1048608 | tf_op jit(solution)/shard_map/all_to_all | solution.py:46
  259.6 7.0 all-to-all-start.6
  269.2 11.2 %all-to-all-done.6 = bf16[8,256,256]{2,0,1:T(8,128)(2,1)} async-done(((bf16[8,256,256]{2,0,1:T(8,128)(2,1)}), bf16[8,256,256]{2,0,1:T(8,128)(2,1)}, u32[]{:S(2)}, u32[]{:S(2)}) %all-to-all-start.6) | async-done | bytes 1048608 | tf_op jit(solution)/shard_map/all_to_all | solution.py:89
  290.4 17.9 %all-to-all-done.9 = bf16[8,32,2048]{2,1,0:T(8,128)(2,1)} async-done(((bf16[8,32,2048]{2,1,0:T(8,128)(2,1)}), bf16[8,32,2048]{2,1,0:T(8,128)(2,1)}, u32[]{:S(2)}, u32[]{:S(2)}) %all-to-all-start.9) | async-done | bytes 1048608 | tf_op jit(solution)/shard_map/all_to_all | solution.py:50
  316.2 10.4 %reshape.479 = f32[8,16,16,256]{2,1,0,3:T(8,128)} reshape(f32[2048,4,8,8]{0,3,2,1:T(8,128)} %copy.111) | data formatting | bytes 4194304 | tf_op jit(solution)/shard_map/div | solution.py:158
  326.7 12.9 %copy.112 = f32[8,16,16,256]{3,2,0,1:T(8,128)} copy(f32[8,16,16,256]{2,1,0,3:T(8,128)} %reshape.479) | data formatting | bytes 4194304 | tf_op jit(solution)/shard_map/div | solution.py:158
  342.3 28.1 %all_to_all.142 = bf16[8,32,2048]{2,1,0:T(8,128)(2,1)S(1)} all-to-all(bf16[8,32,2048]{2,1,0:T(8,128)(2,1)S(1)} %bitcast.258), channel_id=1, replica_groups=mesh['section'=2,'seq'=16,'tensor'=8] {'tensor'}, dimensions={0} | all-to-all | bytes 2097152 | tf_op jit(solution)/shard_map/all_to_all | solution.py:66
  370.9 27.4 %all_to_all.143 = bf16[8,32,2048]{2,1,0:T(8,128)(2,1)S(1)} all-to-all(bf16[8,32,2048]{2,1,0:T(8,128)(2,1)S(1)} %bitcast.260), channel_id=1, replica_groups=mesh['section'=2,'seq'=16,'tensor'=8] {'tensor'}, dimensions={0} | all-to-all | bytes 2097152 | tf_op jit(solution)/shard_map/all_to_all | solution.py:70
  405.0 15.0 %psum.107 = f32[2048]{0:T(1024)S(1)} all-reduce(f32[2048]{0:T(1024)S(1)} %get-tuple-element.26), channel_id=1, replica_groups=mesh['section'=2,'seq'=16,'tensor'=8] {'tensor'}, use_global_device_ids=true, to_apply=%region_5.6 | all-reduce | flops 2048 | bytes 16384 | tf_op jit(solution)/shard_map/psum | solution.py:152
  433.5 20.5 %all-to-all-done.14 = bf16[8,32,2048]{2,1,0:T(8,128)(2,1)} async-done(((bf16[8,32,2048]{2,1,0:T(8,128)(2,1)}), bf16[8,32,2048]{2,1,0:T(8,128)(2,1)}, u32[]{:S(2)}, u32[]{:S(2)}) %all-to-all-start.14) | async-done | bytes 1048608 | tf_op jit(solution)/shard_map/all_to_all | solution.py:46
  454.0 6.9 all-to-all-start.12
  463.6 11.3 %all-to-all-done.12 = bf16[8,256,256]{2,0,1:T(8,128)(2,1)} async-done(((bf16[8,256,256]{2,0,1:T(8,128)(2,1)}), bf16[8,256,256]{2,0,1:T(8,128)(2,1)}, u32[]{:S(2)}, u32[]{:S(2)}) %all-to-all-start.12) | async-done | bytes 1048608 | tf_op jit(solution)/shard_map/all_to_all | solution.py:89
  484.8 18.1 %all-to-all-done.15 = bf16[8,32,2048]{2,1,0:T(8,128)(2,1)} async-done(((bf16[8,32,2048]{2,1,0:T(8,128)(2,1)}), bf16[8,32,2048]{2,1,0:T(8,128)(2,1)}, u32[]{:S(2)}, u32[]{:S(2)}) %all-to-all-start.15) | async-done | bytes 1048608 | tf_op jit(solution)/shard_map/all_to_all | solution.py:50
  510.9 10.4 %reshape.483 = f32[8,16,16,256]{2,1,0,3:T(8,128)} reshape(f32[2048,4,8,8]{0,3,2,1:T(8,128)} %copy.121) | data formatting | bytes 4194304 | tf_op jit(solution)/shard_map/div | solution.py:158
  521.3 12.9 %copy.122 = f32[8,16,16,256]{3,2,0,1:T(8,128)} copy(f32[8,16,16,256]{2,1,0,3:T(8,128)} %reshape.483) | data formatting | bytes 4194304 | tf_op jit(solution)/shard_map/div | solution.py:158
  545.1 6.3 slice.28
  552.8 32.3 %all_gather.18 = bf16[16,2048]{1,0:T(8,128)(2,1)} all-gather(bf16[16,256]{1,0:T(8,128)(2,1)S(1)} %reshape.465), channel_id=1, replica_groups=mesh['section'=2,'seq'=16,'tensor'=8] {'tensor'}, dimensions={1}, use_global_device_ids=true | all-gather | bytes 73728 | tf_op jit(solution)/shard_map/all_gather | solution.py:165
  597.3 34.9 %all_gather.20 = bf16[16,2048]{1,0:T(8,128)(2,1)} all-gather(bf16[16,256]{1,0:T(8,128)(2,1)S(1)} %reshape.467), channel_id=1, replica_groups=mesh['section'=2,'seq'=16,'tensor'=8] {'tensor'}, dimensions={1}, use_global_device_ids=true | all-gather | bytes 73728 | tf_op jit(solution)/shard_map/all_gather | solution.py:165
  639.8 26.5 %all_gather.22 = bf16[16,2048]{1,0:T(8,128)(2,1)} all-gather(bf16[16,256]{1,0:T(8,128)(2,1)S(1)} %reshape.469), channel_id=1, replica_groups=mesh['section'=2,'seq'=16,'tensor'=8] {'tensor'}, dimensions={1}, use_global_device_ids=true | all-gather | bytes 73728 | tf_op jit(solution)/shard_map/all_gather | solution.py:165
  671.2 11.6 %all-gather.6.cloned.1.call-done = bf16[256,2048]{1,0:T(8,128)(2,1)} async-done(((bf16[16,2048]{1,0:T(8,128)(2,1)}), bf16[256,2048]{1,0:T(8,128)(2,1)}) %all-gather.6.cloned.1.call-update) | async-done | bytes 1048592 | tf_op jit(solution)/shard_map/all_gather | solution.py:167
  691.4 40.9 %all-gather.8.cloned.1.call-done = bf16[256,2048]{1,0:T(8,128)(2,1)} async-done(((bf16[16,2048]{1,0:T(8,128)(2,1)}), bf16[256,2048]{1,0:T(8,128)(2,1)}) %all-gather.8.cloned.1.call-update) | async-done | bytes 1048592 | tf_op jit(solution)/shard_map/all_gather | solution.py:167
  734.1 38.7 %all-reduce = (f32[256]{0:T(256)S(1)}, f32[256]{0:T(256)S(1)}, f32[256]{0:T(256)S(1)}, f32[256]{0:T(256)S(1)}, f32[256]{0:T(256)S(1)}, /*index=5*/f32[256]{0:T(256)S(1)}) all-reduce(f32[256]{0:T(256)S(1)} %get-tuple-element.36, f32[256]{0:T(256)S(1)} %get-tuple-element.37, ...), channel_id=1, replica_groups=mesh['section'=2,'seq'=16,'tensor'=8] {'seq'}, use_global_device_ids=true, to_apply=%region_16.17 | all-reduce | flops 1536 | bytes 12288 | tf_op jit(solution)/shard_map/psum | solution.py:178
  772.8 17.7 %all-reduce.1 = (f32[256]{0:T(256)S(1)}, f32[256]{0:T(256)S(1)}, f32[256]{0:T(256)S(1)}, f32[256]{0:T(256)S(1)}, f32[256]{0:T(256)S(1)}, /*index=5*/f32[256]{0:T(256)S(1)}) all-reduce(f32[256]{0:T(256)S(1)} %get-tuple-element.14, f32[256]{0:T(256)S(1)} %get-tuple-element.15, ...), channel_id=1, replica_groups=mesh['section'=2,'seq'=16,'tensor'=8] {'tensor'}, use_global_device_ids=true, to_apply=%region_17.18 | all-reduce | flops 1536 | bytes 12288 | tf_op jit(solution)/shard_map/psum | solution.py:178
  (185 shorter events, 194.0 us)
Async XLA Ops:
  7.2 31.8 %copy-start = (bf16[1,8,256,256]{3,2,1,0:T(8,128)(2,1)S(1)}, bf16[1,8,256,256]{3,2,1,0:T(8,128)(2,1)}, u32[]{:S(2)}) copy-start(bf16[1,8,256,256]{3,2,1,0:T(8,128)(2,1)} %param.12) | copy-start | bytes 3145732
  9.6 22.2 %copy-start.19 = (bf16[256,256]{1,0:T(8,128)(2,1)}, bf16[256,256]{1,0:T(8,128)(2,1)S(1)}, u32[]{:S(2)}) copy-start(bf16[256,256]{1,0:T(8,128)(2,1)S(1)} %mul.236) | copy-start | bytes 393220
  12.3 19.5 %copy-start.26 = (f32[1,256]{1,0:T(1,128)S(1)}, f32[1,256]{1,0:T(1,128)}, u32[]{:S(2)}) copy-start(f32[1,256]{1,0:T(1,128)} %param.11) | copy-start | bytes 3076
  12.9 24.6 %copy-start.1 = (bf16[1,2048,256]{1,2,0:T(8,128)(2,1)}, bf16[1,2048,256]{1,2,0:T(8,128)(2,1)S(1)}, u32[]{:S(2)}) copy-start(bf16[1,2048,256]{1,2,0:T(8,128)(2,1)S(1)} %copy.135) | copy-start | bytes 3145732
  33.3 29.7 %all-to-all-start.2 = ((bf16[8,32,2048]{2,1,0:T(8,128)(2,1)}), bf16[8,32,2048]{2,1,0:T(8,128)(2,1)}, u32[]{:S(2)}, u32[]{:S(2)}) async-start(bf16[8,32,2048]{2,1,0:T(8,128)(2,1)} %bitcast.21), calls=%async_computation.2 | async-start | bytes 2097152 | tf_op jit(solution)/shard_map/all_to_all | solution.py:46
  40.4 29.7 %copy-start.24 = (bf16[1,64,32,32]{1,3,2,0:T(8,128)(2,1)S(1)}, bf16[1,64,32,32]{1,3,2,0:T(8,128)(2,1)}, u32[]{:S(2)}) copy-start(bf16[1,64,32,32]{1,3,2,0:T(8,128)(2,1)} %param.15) | copy-start | bytes 393220
  43.1 27.0 %copy-start.25 = (bf16[1,64,32,32]{1,3,2,0:T(8,128)(2,1)S(1)}, bf16[1,64,32,32]{1,3,2,0:T(8,128)(2,1)}, u32[]{:S(2)}) copy-start(bf16[1,64,32,32]{1,3,2,0:T(8,128)(2,1)} %param.17) | copy-start | bytes 393220
  63.0 20.9 %all-to-all-start = ((bf16[8,256,256]{2,0,1:T(8,128)(2,1)}), bf16[8,256,256]{2,0,1:T(8,128)(2,1)}, u32[]{:S(2)}, u32[]{:S(2)}) async-start(bf16[8,256,256]{2,0,1:T(8,128)(2,1)} %copy.92), calls=%async_computation | async-start | bytes 2097152 | tf_op jit(solution)/shard_map/all_to_all | solution.py:89
  84.0 27.3 %all-to-all-start.3 = ((bf16[8,32,2048]{2,1,0:T(8,128)(2,1)}), bf16[8,32,2048]{2,1,0:T(8,128)(2,1)S(1)}, u32[]{:S(2)}, u32[]{:S(2)}) async-start(bf16[8,32,2048]{2,1,0:T(8,128)(2,1)} %bitcast.247), calls=%async_computation.3 | async-start | bytes 2097152 | tf_op jit(solution)/shard_map/all_to_all | solution.py:50
  90.7 25.6 %copy-start.22 = (bf16[64,4,4,64]{3,2,1,0:T(4,128)(2,1)S(1)}, bf16[64,4,4,64]{3,2,1,0:T(4,128)(2,1)}, u32[]{:S(2)}) copy-start(bf16[64,4,4,64]{3,2,1,0:T(4,128)(2,1)} %get-tuple-element.41) | copy-start | bytes 393220
  111.2 26.8 %all-to-all-start.1 = ((bf16[128,16,256]{2,1,0:T(8,128)(2,1)}), bf16[128,16,256]{2,1,0:T(8,128)(2,1)}, u32[]{:S(2)}, u32[]{:S(2)}) async-start(bf16[128,16,256]{2,1,0:T(8,128)(2,1)} %copy.96), calls=%async_computation.1 | async-start | bytes 2097152 | tf_op jit(solution)/shard_map/all_to_all | solution.py:92
  141.1 30.0 %all-to-all-start.4 = ((bf16[8,32,2048]{2,1,0:T(8,128)(2,1)}), bf16[8,32,2048]{2,1,0:T(8,128)(2,1)}, u32[]{:S(2)}, u32[]{:S(2)}) async-start(bf16[8,32,2048]{2,1,0:T(8,128)(2,1)} %bitcast.250), calls=%async_computation.4 | async-start | bytes 2097152 | tf_op jit(solution)/shard_map/all_to_all | solution.py:66
  203.7 4.5 collective-permute-start
  229.8 29.8 %all-to-all-start.8 = ((bf16[8,32,2048]{2,1,0:T(8,128)(2,1)}), bf16[8,32,2048]{2,1,0:T(8,128)(2,1)}, u32[]{:S(2)}, u32[]{:S(2)}) async-start(bf16[8,32,2048]{2,1,0:T(8,128)(2,1)} %bitcast.251), calls=%async_computation.8 | async-start | bytes 2097152 | tf_op jit(solution)/shard_map/all_to_all | solution.py:46
  259.6 20.8 %all-to-all-start.6 = ((bf16[8,256,256]{2,0,1:T(8,128)(2,1)}), bf16[8,256,256]{2,0,1:T(8,128)(2,1)}, u32[]{:S(2)}, u32[]{:S(2)}) async-start(bf16[8,256,256]{2,0,1:T(8,128)(2,1)} %copy.106), calls=%async_computation.6 | async-start | bytes 2097152 | tf_op jit(solution)/shard_map/all_to_all | solution.py:89
  280.4 27.9 %all-to-all-start.9 = ((bf16[8,32,2048]{2,1,0:T(8,128)(2,1)}), bf16[8,32,2048]{2,1,0:T(8,128)(2,1)}, u32[]{:S(2)}, u32[]{:S(2)}) async-start(bf16[8,32,2048]{2,1,0:T(8,128)(2,1)} %bitcast.248), calls=%async_computation.9 | async-start | bytes 2097152 | tf_op jit(solution)/shard_map/all_to_all | solution.py:50
  308.3 31.3 %all-to-all-start.7 = ((bf16[128,16,256]{2,1,0:T(8,128)(2,1)}), bf16[128,16,256]{2,1,0:T(8,128)(2,1)}, u32[]{:S(2)}, u32[]{:S(2)}) async-start(bf16[128,16,256]{2,1,0:T(8,128)(2,1)} %copy.110), calls=%async_computation.7 | async-start | bytes 2097152 | tf_op jit(solution)/shard_map/all_to_all | solution.py:92
  400.0 3.6 collective-permute-start.1
  424.0 30.1 %all-to-all-start.14 = ((bf16[8,32,2048]{2,1,0:T(8,128)(2,1)}), bf16[8,32,2048]{2,1,0:T(8,128)(2,1)}, u32[]{:S(2)}, u32[]{:S(2)}) async-start(bf16[8,32,2048]{2,1,0:T(8,128)(2,1)} %bitcast.249), calls=%async_computation.14 | async-start | bytes 2097152 | tf_op jit(solution)/shard_map/all_to_all | solution.py:46
  454.0 20.8 %all-to-all-start.12 = ((bf16[8,256,256]{2,0,1:T(8,128)(2,1)}), bf16[8,256,256]{2,0,1:T(8,128)(2,1)}, u32[]{:S(2)}, u32[]{:S(2)}) async-start(bf16[8,256,256]{2,0,1:T(8,128)(2,1)} %copy.116), calls=%async_computation.12 | async-start | bytes 2097152 | tf_op jit(solution)/shard_map/all_to_all | solution.py:89
  474.8 28.1 %all-to-all-start.15 = ((bf16[8,32,2048]{2,1,0:T(8,128)(2,1)}), bf16[8,32,2048]{2,1,0:T(8,128)(2,1)}, u32[]{:S(2)}, u32[]{:S(2)}) async-start(bf16[8,32,2048]{2,1,0:T(8,128)(2,1)} %bitcast.246), calls=%async_computation.15 | async-start | bytes 2097152 | tf_op jit(solution)/shard_map/all_to_all | solution.py:50
  502.9 31.3 %all-to-all-start.13 = ((bf16[128,16,256]{2,1,0:T(8,128)(2,1)}), bf16[128,16,256]{2,1,0:T(8,128)(2,1)}, u32[]{:S(2)}, u32[]{:S(2)}) async-start(bf16[128,16,256]{2,1,0:T(8,128)(2,1)} %copy.120), calls=%async_computation.13 | async-start | bytes 2097152 | tf_op jit(solution)/shard_map/all_to_all | solution.py:92
  537.9 47.3 %all-to-all-start.16 = ((bf16[8,32,2048]{2,1,0:T(8,128)(2,1)}), bf16[8,32,2048]{2,1,0:T(8,128)(2,1)}, u32[]{:S(2)}, u32[]{:S(2)}) async-start(bf16[8,32,2048]{2,1,0:T(8,128)(2,1)} %bitcast.244), calls=%async_computation.16 | async-start | bytes 2097152 | tf_op jit(solution)/shard_map/all_to_all | solution.py:66
  542.2 126.7 %all-gather.4.cloned.1.call-start = ((), (), s32[]{:S(2)}) async-start(), calls=%async_computation.18 | async-start | bytes 1114112 | tf_op jit(solution)/shard_map/all_gather | solution.py:167
  587.9 44.4 %all-to-all-start.17 = ((bf16[8,32,2048]{2,1,0:T(8,128)(2,1)}), bf16[8,32,2048]{2,1,0:T(8,128)(2,1)}, u32[]{:S(2)}, u32[]{:S(2)}) async-start(bf16[8,32,2048]{2,1,0:T(8,128)(2,1)} %bitcast.245), calls=%async_computation.17 | async-start | bytes 2097152 | tf_op jit(solution)/shard_map/all_to_all | solution.py:70
  593.6 89.2 %all-gather.6.cloned.1.call-start = ((), (), s32[]{:S(2)}) async-start(), calls=%async_computation.19 | async-start | bytes 1114112 | tf_op jit(solution)/shard_map/all_gather | solution.py:167
  632.2 100.1 %all-gather.8.cloned.1.call-start = ((), (), s32[]{:S(2)}) async-start(), calls=%async_computation.20 | async-start | bytes 1114112 | tf_op jit(solution)/shard_map/all_gather | solution.py:167
  636.2 30.1 %copy-start.27 = (s32[2,256]{1,0:T(2,128)S(1)}, s32[2,256]{1,0:T(2,128)}, u32[]{:S(2)}) copy-start(s32[2,256]{1,0:T(2,128)} %param.19) | copy-start | bytes 6148
  668.9 16.8 %copy-start.11 = (bf16[2048,256]{0,1:T(8,128)(2,1)S(1)}, bf16[2048,256]{0,1:T(8,128)(2,1)}, u32[]{:S(2)}) copy-start(bf16[2048,256]{0,1:T(8,128)(2,1)} %copy-done.10) | copy-start | bytes 3145732
  668.9 16.8 %copy-start.12 = (bf16[2048,256]{0,1:T(8,128)(2,1)S(1)}, bf16[2048,256]{0,1:T(8,128)(2,1)}, u32[]{:S(2)}) copy-start(bf16[2048,256]{0,1:T(8,128)(2,1)} %fusion.7) | copy-start | bytes 3145732
  687.4 44.9 %copy-start.17 = (bf16[1,2048,256]{2,1,0:T(8,128)(2,1)S(1)}, bf16[1,2048,256]{2,1,0:T(8,128)(2,1)}, u32[]{:S(2)}) copy-start(bf16[1,2048,256]{2,1,0:T(8,128)(2,1)} %param.18) | copy-start | bytes 3145732
  687.4 44.9 %copy-start.23 = (f32[256,256]{0,1:T(8,128)S(1)}, f32[256,256]{0,1:T(8,128)}, u32[]{:S(2)}) copy-start(f32[256,256]{0,1:T(8,128)} %fusion.34) | copy-start | bytes 786436
  (16 other events, 39.9 us)
Sparse Core Ops, SparseCore 0:
  585.3 47.9 all-gather.3
  635.8 47.0 all-gather.5
  685.2 47.0 all-gather.7
